TPU v7x, 512 devices: a whole 4x4x16 slice. The times are simulated.
512 devices in a mesh: dp: 8 (over z_lo), ctx: 64 (over x, z_hi, y, core).
Axes of the slice: x: 4, y: 4, z: 16 (z_hi: 2, z_lo: 8; z = z_hi * 8 + z_lo), core: 2. Of those that a mesh axis runs over, the one named last changes fastest.
Arguments:
- pre_gate: bfloat16 [2048, 16384], P('dp', 'ctx'), may hold values from -6 to 6
- values: bfloat16 [2048, 16384], P('dp', 'ctx'), may hold values from -6 to 6
- post_gate: bfloat16 [2048, 16384], P('dp', 'ctx'), may hold values from -6 to 6
- filters: float32 [256, 16384], P('ctx', 'dp'), may hold values from -0.046875 to 0.046875
- cotangent: bfloat16 [2048, 16384], P('dp', 'ctx'), may hold values from -6 to 6
Outputs:
- mixed: bfloat16 [2048, 16384], P('dp', 'ctx')
- pre_grad: bfloat16 [2048, 16384], P('dp', 'ctx')
- value_grad: bfloat16 [2048, 16384], P('dp', 'ctx')
- post_grad: bfloat16 [2048, 16384], P('dp', 'ctx')
- filter_grad: float32 [256, 16384], P('ctx', 'dp')
All inputs are finite; a program needn't handle non-finite values.
Results may differ from a plain program's by a relative error of at most 0.014.
Values may be sent and summed in bfloat16 or wider, within the bound.
A program may use at most 64 MiB of HBM per device.

v0:
```python
import math

import jax
import jax.numpy as jnp
from jax import lax
from jax.sharding import PartitionSpec as P


def matmul(left, right):
    return jnp.dot(left, right, precision=lax.Precision.HIGHEST, preferred_element_type=jnp.float32)


def contract(form, left, right):
    return jnp.einsum(
        form, left, right, precision=lax.Precision.HIGHEST, preferred_element_type=jnp.float32
    )


def phases(height, width, modulus):
    product = lax.broadcasted_iota(jnp.int32, (height, width), 0) * lax.broadcasted_iota(
        jnp.int32, (height, width), 1
    )
    return (product % modulus).astype(jnp.float32) * (2.0 * math.pi / modulus)


def build_tables(blocks, tokens):
    factor = 1
    for candidate in range(1, tokens + 1):
        if tokens % candidate == 0 and candidate * candidate <= tokens:
            factor = candidate
    second = tokens // factor
    rows = blocks + 1
    total = 2 * blocks * tokens
    first_angle = phases(rows, blocks, 2 * blocks)
    twist_angle = phases(rows, tokens, total)
    inner_angle = phases(factor, factor, factor)
    middle_angle = phases(factor, second, tokens)
    outer_angle = phases(second, second, second)
    back_angle = phases(blocks, rows, 2 * blocks)
    column = lax.broadcasted_iota(jnp.int32, (blocks, rows), 1)
    weight = jnp.where((column == 0) | (column == blocks), 1.0, 2.0).astype(jnp.float32) / total
    return {
        "first_cos": jnp.cos(first_angle),
        "first_nsin": -jnp.sin(first_angle),
        "twist_cos": jnp.cos(twist_angle),
        "twist_sin": jnp.sin(twist_angle),
        "inner_cos": jnp.cos(inner_angle),
        "inner_sin": jnp.sin(inner_angle),
        "middle_cos": jnp.cos(middle_angle),
        "middle_sin": jnp.sin(middle_angle),
        "outer_cos": jnp.cos(outer_angle),
        "outer_sin": jnp.sin(outer_angle),
        "back_cos": weight * jnp.cos(back_angle),
        "back_sin": weight * jnp.sin(back_angle),
    }


def expand(table, ndim):
    return table.reshape((table.shape[0],) + (1,) * (ndim - 2) + (table.shape[1],))


def block_table(cos_part, sin_part):
    return jnp.stack([jnp.stack([cos_part, sin_part]), jnp.stack([-sin_part, cos_part])])


def wave(real_part, imag_part, tables, sign):
    shape = real_part.shape
    factor = tables["inner_cos"].shape[0]
    second = tables["outer_cos"].shape[0]
    stacked = jnp.stack(
        [real_part.reshape(-1, factor, second), imag_part.reshape(-1, factor, second)]
    )
    inner_table = block_table(tables["inner_cos"], sign * tables["inner_sin"])
    middle = contract("prab,pqac->qrcb", stacked, inner_table)
    middle_cos = tables["middle_cos"]
    middle_sin = sign * tables["middle_sin"]
    real_turn = middle[0] * middle_cos - middle[1] * middle_sin
    imag_turn = middle[0] * middle_sin + middle[1] * middle_cos
    turned = jnp.stack([real_turn, imag_turn])
    outer_table = block_table(tables["outer_cos"], sign * tables["outer_sin"])
    result = contract("prcb,pqbd->qrdc", turned, outer_table)
    return (result[0].reshape(shape), result[1].reshape(shape))


def finish_forward(real_first, imag_first, tables):
    ndim = real_first.ndim
    twist_cos = expand(tables["twist_cos"], ndim)
    twist_sin = expand(tables["twist_sin"], ndim)
    real_twist = real_first * twist_cos + imag_first * twist_sin
    imag_twist = imag_first * twist_cos - real_first * twist_sin
    return wave(real_twist, imag_twist, tables, -1.0)


def spectrum(signal, tables):
    flat = signal.reshape(signal.shape[0], -1)
    shape = (tables["first_cos"].shape[0],) + signal.shape[1:]
    real_first = matmul(tables["first_cos"], flat).reshape(shape)
    imag_first = matmul(tables["first_nsin"], flat).reshape(shape)
    return finish_forward(real_first, imag_first, tables)


def inverse_prepare(real_spec, imag_spec, tables):
    ndim = real_spec.ndim
    real_wave, imag_wave = wave(real_spec, imag_spec, tables, 1.0)
    twist_cos = expand(tables["twist_cos"], ndim)
    twist_sin = expand(tables["twist_sin"], ndim)
    real_twist = real_wave * twist_cos - imag_wave * twist_sin
    imag_twist = real_wave * twist_sin + imag_wave * twist_cos
    rows = real_spec.shape[0]
    return (real_twist.reshape(rows, -1), imag_twist.reshape(rows, -1))


def inverse_full(real_spec, imag_spec, tables):
    real_flat, imag_flat = inverse_prepare(real_spec, imag_spec, tables)
    signal = matmul(tables["back_cos"], real_flat) - matmul(tables["back_sin"], imag_flat)
    return signal.reshape((tables["back_cos"].shape[0],) + real_spec.shape[1:])


def body(pre_gate, values, post_gate, filters, cotangent):
    blocks = lax.axis_size("ctx")
    groups = lax.axis_size("dp")
    local_rows = pre_gate.shape[0]
    tokens = pre_gate.shape[1]
    local_filters = filters.shape[0]
    repeats = local_rows // (local_filters * blocks)
    share = blocks // groups
    tables = build_tables(blocks, tokens)
    gated = (pre_gate.astype(jnp.float32) * values.astype(jnp.float32)).astype(jnp.bfloat16)
    conv_grad = (cotangent.astype(jnp.float32) * post_gate.astype(jnp.float32)).astype(jnp.bfloat16)
    gated_blocks = gated.reshape(repeats, blocks, local_filters, tokens)
    grad_blocks = conv_grad.reshape(repeats, blocks, local_filters, tokens)
    tap_local = jnp.transpose(filters.reshape(local_filters, share, tokens), (1, 0, 2))
    piece = lax.all_gather(tap_local, "dp", axis=0, tiled=True)
    count = piece.shape[0]
    flat = piece.reshape(count, -1)
    cos_cols = tables["first_cos"]
    sin_cols = tables["first_nsin"]
    real_first = matmul(cos_cols, flat)
    imag_first = matmul(sin_cols, flat)
    spec_shape = (blocks + 1, 1, local_filters, tokens)
    filt_real, filt_imag = finish_forward(
        real_first.reshape(spec_shape), imag_first.reshape(spec_shape), tables
    )

    def single_spectrum(received):
        return spectrum(received.astype(jnp.float32), tables)

    gated_real, gated_imag = single_spectrum(
        lax.all_to_all(gated_blocks, "ctx", split_axis=1, concat_axis=0, tiled=True)
    )
    prod_real = gated_real * filt_real - gated_imag * filt_imag
    prod_imag = gated_real * filt_imag + gated_imag * filt_real
    result = inverse_full(prod_real, prod_imag, tables).astype(jnp.bfloat16)
    conv_seq = lax.all_to_all(result, "ctx", split_axis=0, concat_axis=1, tiled=True)
    grad_real, grad_imag = single_spectrum(
        lax.all_to_all(grad_blocks, "ctx", split_axis=1, concat_axis=0, tiled=True)
    )
    prod_real = filt_real * grad_real + filt_imag * grad_imag
    prod_imag = filt_real * grad_imag - filt_imag * grad_real
    result = inverse_full(prod_real, prod_imag, tables).astype(jnp.bfloat16)
    gated_seq_grad = lax.all_to_all(result, "ctx", split_axis=0, concat_axis=1, tiled=True)
    cross_real = jnp.sum(gated_real * grad_real + gated_imag * grad_imag, axis=1)
    cross_imag = jnp.sum(gated_real * grad_imag - gated_imag * grad_real, axis=1)
    wave_real, wave_imag = inverse_prepare(cross_real, cross_imag, tables)
    cos_rows = tables["back_cos"]
    sin_rows = tables["back_sin"]
    term = matmul(cos_rows, wave_real) - matmul(sin_rows, wave_imag)
    summed = lax.psum_scatter(
        term.reshape(lax.axis_size("dp") * share, local_filters, tokens).astype(jnp.bfloat16),
        "dp",
        scatter_dimension=0,
        tiled=True,
    ).astype(jnp.float32)
    filter_grad = jnp.transpose(summed, (1, 0, 2)).reshape(local_filters, share * tokens)
    conv_full = conv_seq.reshape(pre_gate.shape).astype(jnp.float32)
    gated_grad = gated_seq_grad.reshape(pre_gate.shape).astype(jnp.float32)
    mixed = (post_gate.astype(jnp.float32) * conv_full).astype(jnp.bfloat16)
    post_grad = (cotangent.astype(jnp.float32) * conv_full).astype(jnp.bfloat16)
    pre_grad = (gated_grad * values.astype(jnp.float32)).astype(jnp.bfloat16)
    value_grad = (gated_grad * pre_gate.astype(jnp.float32)).astype(jnp.bfloat16)
    return (mixed, pre_grad, value_grad, post_grad, filter_grad)


def solution(mesh):
    placed = (P("dp", "ctx"), P("dp", "ctx"), P("dp", "ctx"), P("ctx", "dp"), P("dp", "ctx"))
    return jax.shard_map(
        body,
        mesh=mesh,
        in_specs=placed,
        out_specs=(P("dp", "ctx"), P("dp", "ctx"), P("dp", "ctx"), P("dp", "ctx"), P("ctx", "dp")),
        check_vma=False,
    )
```

profile of v0, /device:TPU:6, one launch (start us, length us, event | category | flops | bytes accessed | tf_op | source)
XLA Modules:
  0.0 358.5 jit_solution(13422068213964474386)
XLA Ops:
  8.9 21.4 %all-to-all-start.2 = ((bf16[1,64,4,256]{3,2,0,1:T(4,128)(2,1)}), bf16[1,64,4,256]{3,2,0,1:T(4,128)(2,1)S(1)}, u32[]{:S(2)}, u32[]{:S(2)}) async-start(bf16[1,64,4,256]{3,2,0,1:T(4,128)(2,1)} %reshape.697), calls=%async_computation.2 | async-start | bytes 262144 | tf_op jit(solution)/shard_map/all_to_all | solution.py:156
  33.0 48.2 %all_gather.3 = f32[64,4,256]{2,1,0:T(4,128)S(1)} all-gather(f32[8,4,256]{2,1,0:T(4,128)} %bitcast.204), channel_id=1, replica_groups=mesh['dp'=8,'ctx'=64] {'dp'}, dimensions={0}, use_global_device_ids=true | all-gather | bytes 294912 | tf_op jit(solution)/shard_map/all_gather | solution.py:133
  85.3 17.0 %all-to-all-start = ((bf16[1,64,4,256]{3,2,0,1:T(4,128)(2,1)}), bf16[1,64,4,256]{3,2,0,1:T(4,128)(2,1)}, u32[]{:S(2)}, u32[]{:S(2)}) async-start(bf16[1,64,4,256]{3,2,0,1:T(4,128)(2,1)} %reshape.689), calls=%async_computation | async-start | bytes 262144 | tf_op jit(solution)/shard_map/all_to_all | solution.py:149
  107.4 1.9 copy.81
  110.0 1.9 copy.83
  114.5 2.7 all-to-all-done
  122.2 1.9 copy.105
  124.1 2.1 reshape.700
  126.2 1.9 copy.107
  129.9 1.9 copy.80
  133.5 1.9 copy.82
  135.4 1.9 multiply_add_fusion.5
  152.6 2.4 copy.126
  159.8 2.4 copy.118
  162.2 2.4 reshape_squeeze.26
  164.5 2.4 copy.119
  166.9 2.3 reshape_squeeze.27
  173.5 14.8 %all-to-all-start.3 = ((bf16[64,1,4,256]{3,2,1,0:T(4,128)(2,1)}), bf16[64,1,4,256]{3,2,1,0:T(4,128)(2,1)S(1)}, u32[]{:S(2)}, u32[]{:S(2)}) async-start(bf16[64,1,4,256]{3,2,1,0:T(4,128)(2,1)} %bitcast.65), calls=%async_computation.3 | async-start | bytes 262144 | tf_op jit(solution)/shard_map/all_to_all | solution.py:161
  190.3 2.4 copy.102
  192.7 2.4 reshape_squeeze.24
  195.0 2.4 copy.103
  197.4 2.3 reshape_squeeze.25
  204.3 17.7 %all-to-all-start.1 = ((bf16[64,1,4,256]{3,2,1,0:T(4,128)(2,1)}), bf16[64,1,4,256]{3,2,1,0:T(4,128)(2,1)S(1)}, u32[]{:S(2)}, u32[]{:S(2)}) async-start(bf16[64,1,4,256]{3,2,1,0:T(4,128)(2,1)} %bitcast.42), calls=%async_computation.1 | async-start | bytes 262144 | tf_op jit(solution)/shard_map/all_to_all | solution.py:154
  225.3 123.2 %all-reduce.3.cloned.1.call-done = bf16[64,4,256]{2,1,0:T(4,128)(2,1)} async-done(((bf16[64,4,256]{2,1,0:T(4,128)(2,1)}), bf16[64,4,256]{2,1,0:T(4,128)(2,1)}) %all-reduce.3.cloned.1.call-update) | async-done | bytes 131088
  (117 shorter events, 61.3 us)
Async XLA Ops:
  8.9 76.4 %all-to-all-start.2 = ((bf16[1,64,4,256]{3,2,0,1:T(4,128)(2,1)}), bf16[1,64,4,256]{3,2,0,1:T(4,128)(2,1)S(1)}, u32[]{:S(2)}, u32[]{:S(2)}) async-start(bf16[1,64,4,256]{3,2,0,1:T(4,128)(2,1)} %reshape.697), calls=%async_computation.2 | async-start | bytes 262144 | tf_op jit(solution)/shard_map/all_to_all | solution.py:156
  85.3 17.5 %copy-start.9 = (bf16[1,64,4,256]{3,2,0,1:T(4,128)(2,1)}, bf16[1,64,4,256]{3,2,0,1:T(4,128)(2,1)S(1)}, u32[]{:S(2)}) copy-start(bf16[1,64,4,256]{3,2,0,1:T(4,128)(2,1)S(1)} %all-to-all-done.2) | copy-start | bytes 393220
  85.3 31.9 %all-to-all-start = ((bf16[1,64,4,256]{3,2,0,1:T(4,128)(2,1)}), bf16[1,64,4,256]{3,2,0,1:T(4,128)(2,1)}, u32[]{:S(2)}, u32[]{:S(2)}) async-start(bf16[1,64,4,256]{3,2,0,1:T(4,128)(2,1)} %reshape.689), calls=%async_computation | async-start | bytes 262144 | tf_op jit(solution)/shard_map/all_to_all | solution.py:149
  104.7 1.9 copy-start.4
  106.7 2.6 copy-start.3
  110.0 2.2 copy-start.10
  135.4 1.9 copy-start.2
  137.3 2.5 copy-start.11
  137.3 2.5 copy-start.13
  143.6 2.5 copy-start.12
  164.5 4.7 %copy-start.14 = (f32[65]{0:T(128)S(1)}, f32[65]{0:T(128)}, u32[]{:S(2)}) copy-start(f32[65]{0:T(128)} %fusion.127) | copy-start | bytes 784
  169.2 19.1 %copy-start = (f32[1,260,16,16]{1,2,3,0:T(8,128)S(1)}, f32[1,260,16,16]{1,2,3,0:T(8,128)}, u32[]{:S(2)}) copy-start(f32[1,260,16,16]{1,2,3,0:T(8,128)} %get-tuple-element.47) | copy-start | bytes 798724
  169.2 19.1 %copy-start.1 = (f32[1,260,16,16]{1,2,3,0:T(8,128)S(1)}, f32[1,260,16,16]{1,2,3,0:T(8,128)}, u32[]{:S(2)}) copy-start(f32[1,260,16,16]{1,2,3,0:T(8,128)} %get-tuple-element.48) | copy-start | bytes 798724
  173.5 30.8 %all-to-all-start.3 = ((bf16[64,1,4,256]{3,2,1,0:T(4,128)(2,1)}), bf16[64,1,4,256]{3,2,1,0:T(4,128)(2,1)S(1)}, u32[]{:S(2)}, u32[]{:S(2)}) async-start(bf16[64,1,4,256]{3,2,1,0:T(4,128)(2,1)} %bitcast.65), calls=%async_computation.3 | async-start | bytes 262144 | tf_op jit(solution)/shard_map/all_to_all | solution.py:161
  203.7 146.1 %copy-start.5 = (bf16[256,256]{1,0:T(8,128)(2,1)S(1)}, bf16[256,256]{1,0:T(8,128)(2,1)}, u32[]{:S(2)}) copy-start(bf16[256,256]{1,0:T(8,128)(2,1)} %param.6) | copy-start | bytes 393220
  203.7 146.1 %copy-start.6 = (bf16[256,256]{1,0:T(8,128)(2,1)S(1)}, bf16[256,256]{1,0:T(8,128)(2,1)}, u32[]{:S(2)}) copy-start(bf16[256,256]{1,0:T(8,128)(2,1)} %param.5) | copy-start | bytes 393220
  204.3 146.4 %copy-start.7 = (bf16[256,256]{1,0:T(8,128)(2,1)S(1)}, bf16[256,256]{1,0:T(8,128)(2,1)}, u32[]{:S(2)}) copy-start(bf16[256,256]{1,0:T(8,128)(2,1)} %param.7) | copy-start | bytes 393220
  204.3 146.4 %copy-start.8 = (bf16[256,256]{1,0:T(8,128)(2,1)S(1)}, bf16[256,256]{1,0:T(8,128)(2,1)}, u32[]{:S(2)}) copy-start(bf16[256,256]{1,0:T(8,128)(2,1)} %param.9) | copy-start | bytes 393220
  204.3 146.3 %all-to-all-start.1 = ((bf16[64,1,4,256]{3,2,1,0:T(4,128)(2,1)}), bf16[64,1,4,256]{3,2,1,0:T(4,128)(2,1)S(1)}, u32[]{:S(2)}, u32[]{:S(2)}) async-start(bf16[64,1,4,256]{3,2,1,0:T(4,128)(2,1)} %bitcast.42), calls=%async_computation.1 | async-start | bytes 262144 | tf_op jit(solution)/shard_map/all_to_all | solution.py:154
  222.0 126.5 %all-reduce.3.cloned.1.call-start = ((), (), s32[]{:S(2)}) async-start(), calls=%async_computation.4 | async-start | bytes 262144
Sparse Core Ops, SparseCore 0:
  226.3 122.1 all-reduce.2
where the time goes:
time: 363 us; the launch traced here: 358 us
  waiting for transfers between devices  126 us (35%)
  starting transfers between devices  71 us (20%)
  local copies, waits for them, and re-layouts  59 us (16%)
  blocking collectives  48.2 us (13%)
  matrix products  24.1 us (7%)
  between operations  15.6 us (4%)
  other arithmetic  14.7 us (4%)
    unnamed x2, waiting for transfers between devices  123 us
    all_gather x1, blocking collectives, body(): piece = lax.all_gather(tap_local, 'dp', axis=0, tiled=True)  48.2 us
    all_to_all x2, starting transfers between devices, body(): lax.all_to_all(result, 'ctx', split_axis=0, concat_axis=1, tiled=True)  32.5 us
    all_to_all x1, starting transfers between devices, body(): lax.all_to_all(grad_blocks, 'ctx', split_axis=1, concat_axis=0, tiled=True)  21.4 us
    all_to_all x1, starting transfers between devices, body(): lax.all_to_all(gated_blocks, 'ctx', split_axis=1, concat_axis=0, tiled=True)  17 us
    slice x9, local copies, waits for them, and re-layouts, wave(): return (result[0].reshape(shape), result[1].reshape(shape))  16.2 us
    dot_general x12, matrix products, matmul(): jnp.dot(left, right, precision=lax.Precision.HIGHEST, preferred_element_t...  13.3 us
    another operation x6, local copies, waits for them, and re-layouts, wave(): return (result[0].reshape(shape), result[1].reshape(shape))  12.7 us
  transfers between devices with their start and end apart: 5, of which 2 were waited for; matrix products, arithmetic and copies ran while one was open for 11% of the time, Pallas kernels for 0%

commit v1 on v0

v1 whole, which is shorter than its diff:
```python
import functools

import jax
import jax.numpy as jnp
import numpy as np
from jax import lax
from jax.experimental import pallas as pl
from jax.experimental.pallas import tpu as pltpu
from jax.sharding import PartitionSpec as P

MESH = pl.DeviceIdType.MESH
BF = jnp.bfloat16
F32 = jnp.float32
ROWS = 8
TOKENS = 256


def tables(nb, groups):
    total = 2 * nb * TOKENS
    k1 = np.arange(nb)[:, None] + 0.5
    angle = 2 * np.pi * k1 * np.arange(nb)[None, :] / (2 * nb)
    first = np.concatenate([np.cos(angle), -np.sin(angle)], axis=0)
    own = nb // groups
    spread = np.repeat(first, ROWS, axis=1)
    column = np.arange(nb * ROWS)
    within = column % (nb * 4)
    block = (within // (own * 4)) * own + (within % (own * 4)) // 4
    filter_spread = first[:, block]
    row = np.arange(nb * 4)
    block_out = (row // (own * 4)) * own + (row % (own * 4)) // 4
    filter_back = first[:, block_out].T
    t = np.arange(TOKENS)
    twist = 2 * np.pi * k1 * t[None, :] / total
    turn = np.stack([np.cos(twist), np.sin(twist)])
    inner = 2 * np.pi * ((t[:, None] * t[None, :]) % TOKENS) / TOKENS
    c, s = np.cos(inner), np.sin(inner)
    third = np.block([[c, -s], [s, c]])
    to = lambda a: np.asarray(a, np.float32).astype(jnp.bfloat16)
    return (
        to(spread),
        to(spread.T),
        to(filter_spread),
        to(filter_back),
        to(third),
        to(third.T),
        np.asarray(turn, np.float32),
    )


def dot(a, b):
    return lax.dot_general(a, b, (((1,), (0,)), ((), ())), preferred_element_type=F32)


def main_kernel(
    nb, groups,
    pre_h, val_h, post_h, cot_h, filt_h, e_h, et_h, ef_h, eft_h, t3_h, t3i_h, tw_h,
    out_h, fgr_h,
    pre, val, post, cot, filt, e, et, ef, eft, t3, t3i, tw,
    xs, recv, fb, w, wt, wf, wtf, a, b, spec, fspec, prod, u, y, sx, rx, fgs,
    in_sem, send_sem, recv_sem,
):
    own = nb // groups
    chunk = own * 4
    half = nb * 4
    dp = lax.axis_index("dp")
    ctx = lax.axis_index("ctx")
    core = lax.rem(ctx, 2)
    chip = lax.div(ctx, 2)
    far = lax.rem(dp + groups // 2, groups)
    partner = ctx + 1 - 2 * core

    pairs = (
        (pre_h, pre), (val_h, val), (post_h, post), (cot_h, cot), (filt_h, filt), (tw_h, tw),
        (e_h, e), (et_h, et), (ef_h, ef), (eft_h, eft), (t3_h, t3), (t3i_h, t3i),
    )
    loads = [pltpu.make_async_copy(s, d, in_sem.at[i]) for i, (s, d) in enumerate(pairs)]
    for load in loads:
        load.start()

    barrier = pltpu.get_barrier_semaphore()

    def greet(j, carry):
        pl.semaphore_signal(barrier, inc=1, device_id={"dp": far, "ctx": j}, device_id_type=MESH)
        return carry

    lax.fori_loop(0, nb, greet, 0)
    pl.semaphore_signal(barrier, inc=1, device_id={"dp": dp, "ctx": partner}, device_id_type=MESH)
    for i in range(1, groups):
        pl.semaphore_signal(
            barrier, inc=1, device_id={"dp": lax.rem(dp + i, groups), "ctx": ctx}, device_id_type=MESH
        )

    for load in loads[:5]:
        load.wait()
    xs[0] = (pre[...].astype(F32) * val[...].astype(F32)).astype(BF)
    xs[1] = (cot[...].astype(F32) * post[...].astype(F32)).astype(BF)
    mine = pl.multiple_of(core * half + dp * chunk, chunk)
    fb[pl.ds(mine, chunk), :] = jnp.concatenate(
        [filt[:, i * TOKENS : (i + 1) * TOKENS] for i in range(own)], axis=0
    ).astype(BF)

    pl.semaphore_wait(barrier, nb + groups)

    for i in range(1, groups):
        pltpu.make_async_remote_copy(
            src_ref=fb.at[pl.ds(mine, chunk), :],
            dst_ref=fb.at[pl.ds(mine, chunk), :],
            send_sem=send_sem.at[0],
            recv_sem=recv_sem.at[0],
            device_id={"dp": lax.rem(dp + i, groups), "ctx": ctx},
            device_id_type=MESH,
        ).start()

    place = pl.multiple_of(ctx * ROWS, ROWS)

    def send_in(m, carry):
        rows = pl.ds(pl.multiple_of(m * ROWS, ROWS), ROWS)
        for signal in range(2):
            pltpu.make_async_remote_copy(
                src_ref=xs.at[signal, rows, :],
                dst_ref=recv.at[pl.ds(place, ROWS), :],
                send_sem=send_sem.at[1],
                recv_sem=recv_sem.at[1],
                device_id={"dp": far, "ctx": 2 * m + signal},
                device_id_type=MESH,
            ).start()
        return carry

    lax.fori_loop(0, nb // 2, send_in, 0)

    for load in loads[5:]:
        load.wait()
    wide = 2 * nb

    def spread_rows(s, carry):
        rows = pl.ds(pl.multiple_of(s * wide, wide), wide)
        column = lax.broadcasted_iota(jnp.int32, (wide, nb * ROWS), 1)
        keep = ((column & (ROWS - 1)) == s).astype(F32)
        w[rows, :] = (e[...].astype(F32) * keep).astype(BF)
        group = jnp.where(column >= half, 4, 0) + (column & 3)
        keep = (group == s).astype(F32)
        wf[rows, :] = (ef[...].astype(F32) * keep).astype(BF)
        return carry

    lax.fori_loop(0, ROWS, spread_rows, 0)
    row = lax.broadcasted_iota(jnp.int32, (nb * ROWS, wide), 0)
    for s in range(ROWS):
        keep = ((row & (ROWS - 1)) == s).astype(F32)
        wt[:, s * wide : (s + 1) * wide] = (et[...].astype(F32) * keep).astype(BF)
    row = lax.broadcasted_iota(jnp.int32, (half, wide), 0)
    for s in range(4):
        keep = ((row & 3) == s).astype(F32)
        wtf[:, s * wide : (s + 1) * wide] = (eft[...].astype(F32) * keep).astype(BF)

    def wait_bytes(ref, sem):
        pltpu.make_async_copy(ref, ref, sem).wait()

    def forward(source, table, result):
        a[...] = dot(table[...], source[...])

        def one(s, carry):
            ar = a[pl.ds(pl.multiple_of(s * wide, wide), nb), :]
            ai = a[pl.ds(pl.multiple_of(s * wide + nb, nb), nb), :]
            tc, ts = tw[0], tw[1]
            rows = pl.ds(pl.multiple_of(s * nb, nb), nb)
            b[rows, 0:TOKENS] = (ar * tc + ai * ts).astype(BF)
            b[rows, TOKENS:] = (ai * tc - ar * ts).astype(BF)
            return carry

        lax.fori_loop(0, ROWS, one, 0)
        result[...] = dot(b[...], t3[...])

    def backward(count):
        spec_rows = count * nb
        v = dot(prod[0:spec_rows, :], t3i[...])
        scale = 2.0 / (2 * nb * TOKENS)
        tc, ts = tw[0] * scale, tw[1] * scale
        for s in range(count):
            vr = v[s * nb : (s + 1) * nb, 0:TOKENS]
            vi = v[s * nb : (s + 1) * nb, TOKENS:]
            u[s * wide : s * wide + nb, :] = (vr * tc - vi * ts).astype(BF)
            u[s * wide + nb : (s + 1) * wide, :] = (vr * ts + vi * tc).astype(BF)

    wait_bytes(fb.at[pl.ds(0, (groups - 1) * chunk), :], recv_sem.at[0])
    side = pl.ds(pl.multiple_of(core * half, half), half)
    swap = pltpu.make_async_remote_copy(
        src_ref=fb.at[side, :],
        dst_ref=fb.at[side, :],
        send_sem=send_sem.at[2],
        recv_sem=recv_sem.at[2],
        device_id={"dp": dp, "ctx": partner},
        device_id_type=MESH,
    )
    swap.start()
    swap.wait()
    forward(fb, wf, fspec)

    wait_bytes(recv, recv_sem.at[1])
    forward(recv, w, spec)

    sign = (1 - 2 * core).astype(F32)
    theirs = pl.ds(pl.multiple_of((1 - core) * half, half), half)
    sx[...] = spec[theirs, :].astype(BF)
    fr, fi = fspec[:, 0:TOKENS], fspec[:, TOKENS:] * sign
    xr, xi = spec[:, 0:TOKENS], spec[:, TOKENS:]
    prod[:, 0:TOKENS] = (fr * xr - fi * xi).astype(BF)
    prod[:, TOKENS:] = (fr * xi + fi * xr).astype(BF)
    cross = pltpu.make_async_remote_copy(
        src_ref=sx,
        dst_ref=rx,
        send_sem=send_sem.at[3],
        recv_sem=recv_sem.at[3],
        device_id={"dp": dp, "ctx": partner},
        device_id_type=MESH,
    )
    cross.start()
    backward(ROWS)
    y[...] = dot(wt[...], u[...]).astype(BF)

    home = pl.ds(pl.multiple_of(chip * ROWS, ROWS), ROWS)

    def send_out(j, carry):
        pltpu.make_async_remote_copy(
            src_ref=y.at[pl.ds(pl.multiple_of(j * ROWS, ROWS), ROWS), :],
            dst_ref=out_h.at[core, home, :],
            send_sem=send_sem.at[4],
            recv_sem=recv_sem.at[4],
            device_id={"dp": far, "ctx": j},
            device_id_type=MESH,
        ).start()
        return carry

    lax.fori_loop(0, nb, send_out, 0)

    cross.wait()
    ours = pl.ds(pl.multiple_of(core * half, half), half)
    xr, xi = spec[ours, 0:TOKENS], spec[ours, TOKENS:]
    gr, gi = rx[:, 0:TOKENS].astype(F32), rx[:, TOKENS:].astype(F32)
    prod[0:half, 0:TOKENS] = (xr * gr + xi * gi).astype(BF)
    prod[0:half, TOKENS:] = ((xr * gi - xi * gr) * sign).astype(BF)
    backward(4)
    fgs[...] = dot(wtf[...], u[0 : 4 * wide, :]).astype(BF)
    here = pl.multiple_of(dp * chunk, chunk)
    keep_own = pltpu.make_async_copy(
        fgs.at[pl.ds(here, chunk), :], fgr_h.at[pl.ds(here, chunk), :], in_sem.at[0]
    )
    keep_own.start()
    for i in range(1, groups):
        peer = lax.rem(dp + i, groups)
        pltpu.make_async_remote_copy(
            src_ref=fgs.at[pl.ds(pl.multiple_of(peer * chunk, chunk), chunk), :],
            dst_ref=fgr_h.at[pl.ds(here, chunk), :],
            send_sem=send_sem.at[5],
            recv_sem=recv_sem.at[5],
            device_id={"dp": peer, "ctx": ctx},
            device_id_type=MESH,
        ).start()

    keep_own.wait()
    others = fb.at[pl.ds(0, (groups - 1) * chunk), :]
    wait_bytes(others, send_sem.at[0])
    wait_bytes(recv, send_sem.at[1])
    wait_bytes(y, send_sem.at[4])
    wait_bytes(others, send_sem.at[5])
    wait_bytes(others, recv_sem.at[5])
    wait_bytes(y, recv_sem.at[4])


def last_kernel(own, groups, pre, val, post, cot, back, fgr, mixed, pre_grad, value_grad, post_grad, filter_grad):
    conv = back[0].astype(F32)
    mixed[...] = (post[...].astype(F32) * conv).astype(BF)
    post_grad[...] = (cot[...].astype(F32) * conv).astype(BF)
    grad = back[1].astype(F32)
    pre_grad[...] = (grad * val[...].astype(F32)).astype(BF)
    value_grad[...] = (grad * pre[...].astype(F32)).astype(BF)
    chunk = own * 4
    total = fgr[0:chunk, :].astype(F32)
    for i in range(1, groups):
        total = total + fgr[i * chunk : (i + 1) * chunk, :].astype(F32)
    for i in range(own):
        filter_grad[:, i * TOKENS : (i + 1) * TOKENS] = total[4 * i : 4 * i + 4, :]


def body(pre_gate, values, post_gate, filters, cotangent):
    nb = lax.axis_size("ctx")
    groups = lax.axis_size("dp")
    own = nb // groups
    rows = nb * 4
    consts = tables(nb, groups)
    anywhere = pl.BlockSpec(memory_space=pl.ANY)
    vmem = pl.BlockSpec(memory_space=pltpu.VMEM)
    sig = (rows, TOKENS)
    scratch = [
        pltpu.VMEM(sig, BF), pltpu.VMEM(sig, BF), pltpu.VMEM(sig, BF), pltpu.VMEM(sig, BF),
        pltpu.VMEM(filters.shape, F32),
        *[pltpu.VMEM(c.shape, BF) for c in consts[:6]],
        pltpu.VMEM(consts[6].shape, F32),
        pltpu.VMEM((2,) + sig, BF),
        pltpu.VMEM((nb * ROWS, TOKENS), BF),
        pltpu.VMEM((nb * ROWS, TOKENS), BF),
        pltpu.VMEM((ROWS * 2 * nb, nb * ROWS), BF),
        pltpu.VMEM((nb * ROWS, ROWS * 2 * nb), BF),
        pltpu.VMEM((ROWS * 2 * nb, nb * ROWS), BF),
        pltpu.VMEM((nb * 4, 4 * 2 * nb), BF),
        pltpu.VMEM((ROWS * 2 * nb, TOKENS), F32),
        pltpu.VMEM((ROWS * nb, 2 * TOKENS), BF),
        pltpu.VMEM((ROWS * nb, 2 * TOKENS), F32),
        pltpu.VMEM((ROWS * nb, 2 * TOKENS), F32),
        pltpu.VMEM((ROWS * nb, 2 * TOKENS), BF),
        pltpu.VMEM((ROWS * 2 * nb, TOKENS), BF),
        pltpu.VMEM((nb * ROWS, TOKENS), BF),
        pltpu.VMEM((4 * nb, 2 * TOKENS), BF),
        pltpu.VMEM((4 * nb, 2 * TOKENS), BF),
        pltpu.VMEM((nb * 4, TOKENS), BF),
        pltpu.SemaphoreType.DMA((12,)),
        pltpu.SemaphoreType.DMA((6,)),
        pltpu.SemaphoreType.DMA((6,)),
    ]
    back, fgr = pl.pallas_call(
        functools.partial(main_kernel, nb, groups),
        out_shape=(jax.ShapeDtypeStruct((2,) + sig, BF), jax.ShapeDtypeStruct(sig, BF)),
        in_specs=[anywhere] * 12,
        out_specs=(anywhere, anywhere),
        scratch_shapes=scratch,
        compiler_params=pltpu.CompilerParams(collective_id=0, has_side_effects=True),
        name="long_conv",
    )(pre_gate, values, post_gate, cotangent, filters, *consts)
    shape = jax.ShapeDtypeStruct(pre_gate.shape, BF)
    mixed, pre_grad, value_grad, post_grad, filter_grad = pl.pallas_call(
        functools.partial(last_kernel, own, groups),
        out_shape=(shape, shape, shape, shape, jax.ShapeDtypeStruct(filters.shape, F32)),
        in_specs=[vmem] * 6,
        out_specs=(vmem,) * 5,
        name="gates",
    )(pre_gate, values, post_gate, cotangent, back, fgr)
    return (mixed, pre_grad, value_grad, post_grad, filter_grad)


def solution(mesh):
    big = P("dp", "ctx")
    return jax.shard_map(
        body,
        mesh=mesh,
        in_specs=(big, big, big, P("ctx", "dp"), big),
        out_specs=(big, big, big, big, P("ctx", "dp")),
        check_vma=False,
    )
```

time: 363 us -> 61.7 us (0.17)
  waiting for transfers between devices: 126 us -> 0 us
  starting transfers between devices: 71 us -> 0 us
  Pallas kernels: 0 us -> 59.9 us
  local copies, waits for them, and re-layouts: 59 us -> 0 us
  blocking collectives: 48.2 us -> 0 us
  matrix products: 24.1 us -> 0 us
  between operations: 15.6 us -> 0.64 us
  other arithmetic: 14.7 us -> 0 us
    unnamed x2 -> x0, waiting for transfers between devices: 123 us -> none
    all_to_all x4 -> x0, starting transfers between devices: 70.9 us -> none  [the longest x2 32.5 us: body(): lax.all_to_all(result, 'ctx', split_axis=0, concat_axis=1, tiled=True)]
    pallas_call x0 -> x2, Pallas kernels: none -> 59.9 us  [the longest x1 57.8 us: body(): pl.pallas_call(functools.partial(main_kernel, nb, groups), out_shape=(jax...]
    all_gather x1 -> x0, blocking collectives: 48.2 us -> none  [body(): piece = lax.all_gather(tap_local, 'dp', axis=0, tiled=True)]
    dot_general x24 -> x0, matrix products: 24.1 us -> none  [the longest x12 13.3 us: matmul(): jnp.dot(left, right, precision=lax.Precision.HIGHEST, preferred_element_t...]
    reshape x14 -> x0, local copies, waits for them, and re-layouts: 20 us -> none  [the longest x4 7.65 us: spectrum(): imag_first = matmul(tables['first_nsin'], flat).reshape(shape)]
    slice x9 -> x0, local copies, waits for them, and re-layouts: 16.2 us -> none  [wave(): return (result[0].reshape(shape), result[1].reshape(shape))]
    another operation x6 -> x0, local copies, waits for them, and re-layouts: 12.7 us -> none  [wave(): return (result[0].reshape(shape), result[1].reshape(shape))]
  transfers between devices with their start and end apart: 5 -> 0, of which waited for: 2 -> 0; matrix products, arithmetic and copies ran while one was open for 11% -> 0% of each run, Pallas kernels for 0% -> 0%
where the time goes in v1:
time: 61.7 us; the launch traced here: 60.5 us
  Pallas kernels  59.9 us (97%)
  between operations  0.64 us (1%)
    pallas_call x1, Pallas kernels, body(): pl.pallas_call(functools.partial(main_kernel, nb, groups), out_shape=(jax...  57.8 us
    pallas_call x1, Pallas kernels, body(): pl.pallas_call(functools.partial(last_kernel, own, groups), out_shape=(sh...  2.07 us

profile of v1, /device:TPU:6, one launch (start us, length us, event | category | flops | bytes accessed | tf_op | source)
XLA Modules:
  0.0 60.5 jit_solution(8567187459042093263)
XLA Ops:
  0.6 57.8 %long_conv.1 = (bf16[2,256,256]{2,1,0:T(8,128)(2,1)}, bf16[256,256]{1,0:T(8,128)(2,1)}) custom-call(bf16[256,256]{1,0:T(8,128)(2,1)} %pre.1, bf16[256,256]{1,0:T(8,128)(2,1)} %val.1, bf16[256,256]{1,0:T(8,128)(2,1)} %post.1, bf16[256,256]{1,0:T(8,128)(2,1)} %cot.1, f32[4,2048]{1,0:T(4,128)} %filt_h.1, bf16[128,512]{1,0:T(8,128)(2,1)} %constant.14.clone.e_h, ...), custom_call_target="tpu_custom_call" | custom-call | tf_op jit(solution)/shard_map/long_conv/pallas_call | solution.py:319
  58.5 2.1 %gates.1 = (bf16[256,256]{1,0:T(8,128)(2,1)}, bf16[256,256]{1,0:T(8,128)(2,1)}, bf16[256,256]{1,0:T(8,128)(2,1)}, bf16[256,256]{1,0:T(8,128)(2,1)}, f32[4,2048]{1,0:T(4,128)}) custom-call(bf16[256,256]{1,0:T(8,128)(2,1)} %pre.1, bf16[256,256]{1,0:T(8,128)(2,1)} %val.1, bf16[256,256]{1,0:T(8,128)(2,1)} %post.1, bf16[256,256]{1,0:T(8,128)(2,1)} %cot.1, ...), custom_call_target="tpu_custom_call" | custom-call | tf_op jit(solution)/shard_map/gates/pallas_call | solution.py:329

commit v2 on v1

--- a/solution.py
+++ b/solution.py
@@ -22,13 +22,12 @@
     first = np.concatenate([np.cos(angle), -np.sin(angle)], axis=0)
     own = nb // groups
     spread = np.repeat(first, ROWS, axis=1)
-    column = np.arange(nb * ROWS)
-    within = column % (nb * 4)
-    block = (within // (own * 4)) * own + (within % (own * 4)) // 4
-    filter_spread = first[:, block]
     row = np.arange(nb * 4)
-    block_out = (row // (own * 4)) * own + (row % (own * 4)) // 4
-    filter_back = first[:, block_out].T
+    place, inside = row // (own * 4), row % (own * 4)
+    lags = 2 * (place % (groups // 2)) + place // (groups // 2)
+    block = lags * own + inside // 4
+    filter_spread = np.tile(first[:, block], (1, 2))
+    filter_back = first[:, block].T
     t = np.arange(TOKENS)
     twist = 2 * np.pi * k1 * t[None, :] / total
     turn = np.stack([np.cos(twist), np.sin(twist)])
@@ -56,7 +55,7 @@
     pre_h, val_h, post_h, cot_h, filt_h, e_h, et_h, ef_h, eft_h, t3_h, t3i_h, tw_h,
     out_h, fgr_h,
     pre, val, post, cot, filt, e, et, ef, eft, t3, t3i, tw,
-    xs, recv, fb, w, wt, wf, wtf, a, b, spec, fspec, prod, u, y, sx, rx, fgs,
+    xs, recv, fb, w, wt, wf, wtf, a, b, spec, fspec, prod, u, y, sx, rx, fgs, fgf, fgn, fgt,
     in_sem, send_sem, recv_sem,
 ):
     own = nb // groups
@@ -68,6 +67,10 @@
     chip = lax.div(ctx, 2)
     far = lax.rem(dp + groups // 2, groups)
     partner = ctx + 1 - 2 * core
+    parity = lax.rem(dp, 2)
+    near = dp + 1 - 2 * parity
+    rank = lax.div(dp, 2)
+    quarter = half // 2
 
     pairs = (
         (pre_h, pre), (val_h, val), (post_h, post), (cot_h, cot), (filt_h, filt), (tw_h, tw),
@@ -85,7 +88,10 @@
 
     lax.fori_loop(0, nb, greet, 0)
     pl.semaphore_signal(barrier, inc=1, device_id={"dp": dp, "ctx": partner}, device_id_type=MESH)
-    for i in range(1, groups):
+    pl.semaphore_signal(barrier, inc=1, device_id={"dp": near, "ctx": ctx}, device_id_type=MESH)
+    even = [i for i in range(2, groups, 2)]
+    greeted = [i for i in even if i != groups // 2]
+    for i in greeted:
         pl.semaphore_signal(
             barrier, inc=1, device_id={"dp": lax.rem(dp + i, groups), "ctx": ctx}, device_id_type=MESH
         )
@@ -94,14 +100,17 @@
         load.wait()
     xs[0] = (pre[...].astype(F32) * val[...].astype(F32)).astype(BF)
     xs[1] = (cot[...].astype(F32) * post[...].astype(F32)).astype(BF)
-    mine = pl.multiple_of(core * half + dp * chunk, chunk)
+    mine = pl.multiple_of(core * half + parity * quarter + rank * chunk, chunk)
     fb[pl.ds(mine, chunk), :] = jnp.concatenate(
         [filt[:, i * TOKENS : (i + 1) * TOKENS] for i in range(own)], axis=0
     ).astype(BF)
 
-    pl.semaphore_wait(barrier, nb + groups)
-
-    for i in range(1, groups):
+    pl.semaphore_wait(barrier, nb + 2 + len(greeted))
+
+    def wait_bytes(ref, sem):
+        pltpu.make_async_copy(ref, ref, sem).wait()
+
+    for i in even:
         pltpu.make_async_remote_copy(
             src_ref=fb.at[pl.ds(mine, chunk), :],
             dst_ref=fb.at[pl.ds(mine, chunk), :],
@@ -113,9 +122,9 @@
 
     place = pl.multiple_of(ctx * ROWS, ROWS)
 
-    def send_in(m, carry):
-        rows = pl.ds(pl.multiple_of(m * ROWS, ROWS), ROWS)
-        for signal in range(2):
+    def send_rows(signal):
+        def one(m, carry):
+            rows = pl.ds(pl.multiple_of(m * ROWS, ROWS), ROWS)
             pltpu.make_async_remote_copy(
                 src_ref=xs.at[signal, rows, :],
                 dst_ref=recv.at[pl.ds(place, ROWS), :],
@@ -124,9 +133,11 @@
                 device_id={"dp": far, "ctx": 2 * m + signal},
                 device_id_type=MESH,
             ).start()
-        return carry
-
-    lax.fori_loop(0, nb // 2, send_in, 0)
+            return carry
+
+        lax.fori_loop(0, nb // 2, one, 0)
+
+    send_rows(0)
 
     for load in loads[5:]:
         load.wait()
@@ -143,6 +154,22 @@
         return carry
 
     lax.fori_loop(0, ROWS, spread_rows, 0)
+
+    if even:
+        wait_bytes(fb.at[pl.ds(0, len(even) * chunk), :], recv_sem.at[0])
+    known = pl.ds(pl.multiple_of(core * half + parity * quarter, quarter), quarter)
+    pass_on = pltpu.make_async_remote_copy(
+        src_ref=fb.at[known, :],
+        dst_ref=fb.at[known, :],
+        send_sem=send_sem.at[6],
+        recv_sem=recv_sem.at[6],
+        device_id={"dp": near, "ctx": ctx},
+        device_id_type=MESH,
+    )
+    pass_on.start()
+    wait_bytes(xs.at[0], send_sem.at[1])
+    send_rows(1)
+
     row = lax.broadcasted_iota(jnp.int32, (nb * ROWS, wide), 0)
     for s in range(ROWS):
         keep = ((row & (ROWS - 1)) == s).astype(F32)
@@ -151,9 +178,6 @@
     for s in range(4):
         keep = ((row & 3) == s).astype(F32)
         wtf[:, s * wide : (s + 1) * wide] = (eft[...].astype(F32) * keep).astype(BF)
-
-    def wait_bytes(ref, sem):
-        pltpu.make_async_copy(ref, ref, sem).wait()
 
     def forward(source, table, result):
         a[...] = dot(table[...], source[...])
@@ -181,7 +205,7 @@
             u[s * wide : s * wide + nb, :] = (vr * tc - vi * ts).astype(BF)
             u[s * wide + nb : (s + 1) * wide, :] = (vr * ts + vi * tc).astype(BF)
 
-    wait_bytes(fb.at[pl.ds(0, (groups - 1) * chunk), :], recv_sem.at[0])
+    pass_on.wait()
     side = pl.ds(pl.multiple_of(core * half, half), half)
     swap = pltpu.make_async_remote_copy(
         src_ref=fb.at[side, :],
@@ -239,16 +263,30 @@
     prod[0:half, 0:TOKENS] = (xr * gr + xi * gi).astype(BF)
     prod[0:half, TOKENS:] = ((xr * gi - xi * gr) * sign).astype(BF)
     backward(4)
-    fgs[...] = dot(wtf[...], u[0 : 4 * wide, :]).astype(BF)
-    here = pl.multiple_of(dp * chunk, chunk)
+    fg = dot(wtf[...], u[0 : 4 * wide, :])
+    fgf[...] = fg
+    fgs[...] = fg.astype(BF)
+    hop = pltpu.make_async_remote_copy(
+        src_ref=fgs.at[pl.ds(pl.multiple_of((1 - parity) * quarter, quarter), quarter), :],
+        dst_ref=fgn,
+        send_sem=send_sem.at[7],
+        recv_sem=recv_sem.at[7],
+        device_id={"dp": near, "ctx": ctx},
+        device_id_type=MESH,
+    )
+    hop.start()
+    hop.wait()
+    kept = fgf[pl.ds(pl.multiple_of(parity * quarter, quarter), quarter), :]
+    fgt[...] = (kept + fgn[...].astype(F32)).astype(BF)
+    here = pl.multiple_of(rank * chunk, chunk)
     keep_own = pltpu.make_async_copy(
-        fgs.at[pl.ds(here, chunk), :], fgr_h.at[pl.ds(here, chunk), :], in_sem.at[0]
+        fgt.at[pl.ds(here, chunk), :], fgr_h.at[pl.ds(here, chunk), :], in_sem.at[0]
     )
     keep_own.start()
-    for i in range(1, groups):
+    for i in even:
         peer = lax.rem(dp + i, groups)
         pltpu.make_async_remote_copy(
-            src_ref=fgs.at[pl.ds(pl.multiple_of(peer * chunk, chunk), chunk), :],
+            src_ref=fgt.at[pl.ds(pl.multiple_of(lax.div(peer, 2) * chunk, chunk), chunk), :],
             dst_ref=fgr_h.at[pl.ds(here, chunk), :],
             send_sem=send_sem.at[5],
             recv_sem=recv_sem.at[5],
@@ -257,12 +295,13 @@
         ).start()
 
     keep_own.wait()
-    others = fb.at[pl.ds(0, (groups - 1) * chunk), :]
-    wait_bytes(others, send_sem.at[0])
-    wait_bytes(recv, send_sem.at[1])
+    if even:
+        others = fb.at[pl.ds(0, len(even) * chunk), :]
+        wait_bytes(others, send_sem.at[0])
+        wait_bytes(others, send_sem.at[5])
+        wait_bytes(others, recv_sem.at[5])
+    wait_bytes(xs.at[1], send_sem.at[1])
     wait_bytes(y, send_sem.at[4])
-    wait_bytes(others, send_sem.at[5])
-    wait_bytes(others, recv_sem.at[5])
     wait_bytes(y, recv_sem.at[4])
 
 
@@ -275,7 +314,7 @@
     value_grad[...] = (grad * pre[...].astype(F32)).astype(BF)
     chunk = own * 4
     total = fgr[0:chunk, :].astype(F32)
-    for i in range(1, groups):
+    for i in range(1, groups // 2):
         total = total + fgr[i * chunk : (i + 1) * chunk, :].astype(F32)
     for i in range(own):
         filter_grad[:, i * TOKENS : (i + 1) * TOKENS] = total[4 * i : 4 * i + 4, :]
@@ -312,13 +351,16 @@
         pltpu.VMEM((4 * nb, 2 * TOKENS), BF),
         pltpu.VMEM((4 * nb, 2 * TOKENS), BF),
         pltpu.VMEM((nb * 4, TOKENS), BF),
+        pltpu.VMEM((nb * 4, TOKENS), F32),
+        pltpu.VMEM((nb * 2, TOKENS), BF),
+        pltpu.VMEM((nb * 2, TOKENS), BF),
         pltpu.SemaphoreType.DMA((12,)),
-        pltpu.SemaphoreType.DMA((6,)),
-        pltpu.SemaphoreType.DMA((6,)),
+        pltpu.SemaphoreType.DMA((8,)),
+        pltpu.SemaphoreType.DMA((8,)),
     ]
     back, fgr = pl.pallas_call(
         functools.partial(main_kernel, nb, groups),
-        out_shape=(jax.ShapeDtypeStruct((2,) + sig, BF), jax.ShapeDtypeStruct(sig, BF)),
+        out_shape=(jax.ShapeDtypeStruct((2,) + sig, BF), jax.ShapeDtypeStruct((nb * 2, TOKENS), BF)),
         in_specs=[anywhere] * 12,
         out_specs=(anywhere, anywhere),
         scratch_shapes=scratch,

time: 61.7 us -> 61.6 us (level)
  the two profiles are of different devices: /device:TPU:6 before, /device:TPU:32 now
where the time goes in v2:
time: 61.6 us; the launch traced here: 61.4 us
  Pallas kernels  60.8 us (99%)
  between operations  0.64 us (1%)
    pallas_call x1, Pallas kernels, body(): pl.pallas_call(functools.partial(main_kernel, nb, groups), out_shape=(jax...  58.8 us
    pallas_call x1, Pallas kernels, body(): pl.pallas_call(functools.partial(last_kernel, own, groups), out_shape=(sh...  2.04 us

profile of v2, /device:TPU:32, one launch (start us, length us, event | category | flops | bytes accessed | tf_op | source)
XLA Modules:
  0.0 61.4 jit_solution(7105556714061188945)
XLA Ops:
  0.6 58.8 %long_conv.1 = (bf16[2,256,256]{2,1,0:T(8,128)(2,1)}, bf16[128,256]{1,0:T(8,128)(2,1)}) custom-call(bf16[256,256]{1,0:T(8,128)(2,1)} %pre.1, bf16[256,256]{1,0:T(8,128)(2,1)} %val.1, bf16[256,256]{1,0:T(8,128)(2,1)} %post.1, bf16[256,256]{1,0:T(8,128)(2,1)} %cot.1, f32[4,2048]{1,0:T(4,128)} %filt_h.1, bf16[128,512]{1,0:T(8,128)(2,1)} %constant.14.clone.e_h, ...), custom_call_target="tpu_custom_call" | custom-call | tf_op jit(solution)/shard_map/long_conv/pallas_call | solution.py:361
  59.4 2.0 %gates.1 = (bf16[256,256]{1,0:T(8,128)(2,1)}, bf16[256,256]{1,0:T(8,128)(2,1)}, bf16[256,256]{1,0:T(8,128)(2,1)}, bf16[256,256]{1,0:T(8,128)(2,1)}, f32[4,2048]{1,0:T(4,128)}) custom-call(bf16[256,256]{1,0:T(8,128)(2,1)} %pre.1, bf16[256,256]{1,0:T(8,128)(2,1)} %val.1, bf16[256,256]{1,0:T(8,128)(2,1)} %post.1, bf16[256,256]{1,0:T(8,128)(2,1)} %cot.1, ...), custom_call_target="tpu_custom_call" | custom-call | tf_op jit(solution)/shard_map/gates/pallas_call | solution.py:371

commit v3 on v1

v3 whole, which is shorter than its diff:
```python
import functools

import jax
import jax.numpy as jnp
import numpy as np
from jax import lax
from jax.experimental import pallas as pl
from jax.experimental.pallas import tpu as pltpu
from jax.sharding import PartitionSpec as P

MESH = pl.DeviceIdType.MESH
BF = jnp.bfloat16
F32 = jnp.float32
ROWS = 8
TOKENS = 256


def tables(nb, groups):
    total = 2 * nb * TOKENS
    k1 = np.arange(nb)[:, None] + 0.5
    angle = 2 * np.pi * k1 * np.arange(nb)[None, :] / (2 * nb)
    first = np.concatenate([np.cos(angle), -np.sin(angle)], axis=0)
    spread = np.repeat(first, ROWS, axis=1)
    filter_spread = np.repeat(first, 4, axis=1)
    filter_back = np.repeat(first, 2, axis=1).T
    t = np.arange(TOKENS)
    twist = 2 * np.pi * k1 * t[None, :] / total
    turn = np.stack([np.cos(twist), np.sin(twist)])
    inner = 2 * np.pi * ((t[:, None] * t[None, :]) % TOKENS) / TOKENS
    c, s = np.cos(inner), np.sin(inner)
    third = np.block([[c, -s], [s, c]])
    to = lambda a: np.asarray(a, np.float32).astype(jnp.bfloat16)
    return (
        to(spread),
        to(spread.T),
        to(filter_spread),
        to(filter_back),
        to(third),
        to(third.T),
        np.asarray(turn, np.float32),
    )


def dot(a, b):
    return lax.dot_general(a, b, (((1,), (0,)), ((), ())), preferred_element_type=F32)


def main_kernel(
    nb, groups,
    pre_h, val_h, post_h, cot_h, filt_h, e_h, et_h, ef_h, eft_h, t3_h, t3i_h, tw_h,
    out_h, fgr_h,
    pre, val, post, cot, filt, e, et, ef, eft, t3, t3i, tw,
    xs, recv, fbs, fb, w, wt, wf, wtf, a, b, spec, fspec, prod, u, y, sx, rx, fgs,
    in_sem, send_sem, recv_sem, row_sem,
):
    own = nb // groups
    chunk = own * 4
    piece = own * 2
    wide = 2 * nb
    dp = lax.axis_index("dp")
    ctx = lax.axis_index("ctx")
    core = lax.rem(ctx, 2)
    chip = lax.div(ctx, 2)
    parity = lax.rem(dp, 2)
    base = dp - parity
    far = lax.rem(base + groups // 2, groups)
    rank = lax.div(dp, 2)
    partner = ctx + 1 - 2 * core
    holder = core == parity

    barrier = pltpu.get_barrier_semaphore()

    def greet(j, carry):
        for part in range(2):
            pl.semaphore_signal(barrier, inc=1, device_id={"dp": far + part, "ctx": j}, device_id_type=MESH)
        return carry

    lax.fori_loop(0, nb, greet, 0)
    line = [(dp, partner)]
    for side in range(2):
        line.append((base + 1 - parity, 2 * chip + side))
        for i in range(2, groups):
            if i // 2 != groups // 4:
                line.append((lax.rem(base + i, groups), 2 * chip + side))
    for place, seat in line:
        pl.semaphore_signal(barrier, inc=1, device_id={"dp": place, "ctx": seat}, device_id_type=MESH)
    greeted = 2 * nb + len(line)

    pairs = (
        (pre_h, pre), (val_h, val), (post_h, post), (cot_h, cot), (filt_h, filt), (tw_h, tw),
        (e_h, e), (et_h, et), (ef_h, ef), (eft_h, eft), (t3_h, t3), (t3i_h, t3i),
    )
    loads = [pltpu.make_async_copy(s, d, in_sem.at[i]) for i, (s, d) in enumerate(pairs)]
    for load in loads:
        load.start()
    for load in loads[:5]:
        load.wait()
    xs[0] = (pre[...].astype(F32) * val[...].astype(F32)).astype(BF)
    xs[1] = (cot[...].astype(F32) * post[...].astype(F32)).astype(BF)
    lags = jnp.concatenate(
        [filt[:, i * TOKENS : (i + 1) * TOKENS] for i in range(own)], axis=0
    ).astype(BF)
    fbs[...] = lags
    mine = pl.multiple_of(dp * chunk, chunk)

    @pl.when(holder)
    def _():
        fb[pl.ds(mine, chunk), :] = lags

    pl.semaphore_wait(barrier, greeted)

    def wait_bytes(ref, sem):
        pltpu.make_async_copy(ref, ref, sem).wait()

    for k in range(groups // 2):
        place = core + 2 * k

        @pl.when(place != dp)
        def _():
            pltpu.make_async_remote_copy(
                src_ref=fbs,
                dst_ref=fb.at[pl.ds(mine, chunk), :],
                send_sem=send_sem.at[0],
                recv_sem=recv_sem.at[0],
                device_id={"dp": place, "ctx": ctx},
                device_id_type=MESH,
            ).start()

    landing = pl.ds(pl.multiple_of(ctx * ROWS + parity * 4, 4), 4)

    def row(m, part, signal, sem):
        return pltpu.make_async_remote_copy(
            src_ref=xs.at[signal, pl.ds(pl.multiple_of(m * ROWS + 4 * part, 4), 4), :],
            dst_ref=recv.at[landing, :],
            send_sem=sem,
            recv_sem=recv_sem.at[1],
            device_id={"dp": far + part, "ctx": 2 * m + signal},
            device_id_type=MESH,
        )

    def send_first(m, carry):
        for part in range(2):
            row(m, part, 0, row_sem.at[2 * m + part]).start()
        return carry

    def send_second(m, carry):
        for part in range(2):
            row(m, part, 0, row_sem.at[2 * m + part]).wait_send()
            row(m, part, 1, send_sem.at[1]).start()
        return carry

    lax.fori_loop(0, nb // 2, send_first, 0)

    for load in loads[5:]:
        load.wait()
    column = lax.broadcasted_iota(jnp.int32, (wide, nb * ROWS), 1)
    for s in range(ROWS):
        keep = ((column & (ROWS - 1)) == s).astype(F32)
        w[s * wide : (s + 1) * wide, :] = (e[...].astype(F32) * keep).astype(BF)
    column = lax.broadcasted_iota(jnp.int32, (wide, nb * 4), 1)
    for s in range(4):
        keep = ((column & 3) == s).astype(F32)
        wf[s * wide : (s + 1) * wide, :] = (ef[...].astype(F32) * keep).astype(BF)
    lax.fori_loop(0, nb // 2, send_second, 0)
    at = lax.broadcasted_iota(jnp.int32, (nb * ROWS, wide), 0)
    for s in range(ROWS):
        keep = ((at & (ROWS - 1)) == s).astype(F32)
        wt[:, s * wide : (s + 1) * wide] = (et[...].astype(F32) * keep).astype(BF)
    at = lax.broadcasted_iota(jnp.int32, (nb * 2, wide), 0)
    for s in range(2):
        keep = ((at & 1) == s).astype(F32)
        wtf[:, s * wide : (s + 1) * wide] = (eft[...].astype(F32) * keep).astype(BF)

    def forward(count, source, table, result):
        a[0 : count * wide, :] = dot(table[...], source[...])

        def one(s, carry):
            ar = a[pl.ds(pl.multiple_of(s * wide, wide), nb), :]
            ai = a[pl.ds(pl.multiple_of(s * wide + nb, nb), nb), :]
            tc, ts = tw[0], tw[1]
            rows = pl.ds(pl.multiple_of(s * nb, nb), nb)
            b[rows, 0:TOKENS] = (ar * tc + ai * ts).astype(BF)
            b[rows, TOKENS:] = (ai * tc - ar * ts).astype(BF)
            return carry

        lax.fori_loop(0, count, one, 0)
        result[...] = dot(b[0 : count * nb, :], t3[...])

    def backward(count):
        v = dot(prod[0 : count * nb, :], t3i[...])
        scale = 2.0 / (2 * nb * TOKENS)
        tc, ts = tw[0] * scale, tw[1] * scale
        for s in range(count):
            vr = v[s * nb : (s + 1) * nb, 0:TOKENS]
            vi = v[s * nb : (s + 1) * nb, TOKENS:]
            u[s * wide : s * wide + nb, :] = (vr * tc - vi * ts).astype(BF)
            u[s * wide + nb : (s + 1) * wide, :] = (vr * ts + vi * tc).astype(BF)

    swap = pltpu.make_async_remote_copy(
        src_ref=fb,
        dst_ref=fb,
        send_sem=send_sem.at[2],
        recv_sem=recv_sem.at[2],
        device_id={"dp": dp, "ctx": partner},
        device_id_type=MESH,
    )

    @pl.when(holder)
    def _():
        wait_bytes(fb.at[pl.ds(0, (groups - 1) * chunk), :], recv_sem.at[0])
        swap.start()

    @pl.when(jnp.logical_not(holder))
    def _():
        swap.wait_recv()

    forward(4, fb, wf, fspec)

    wait_bytes(recv, recv_sem.at[1])
    forward(ROWS, recv, w, spec)

    sign = (1 - 2 * core).astype(F32)
    two = 2 * nb
    four = 4 * nb
    theirs = pl.multiple_of((1 - core) * two, two)
    sx[0:two, :] = spec[pl.ds(theirs, two), :].astype(BF)
    sx[two:, :] = spec[pl.ds(four + theirs, two), :].astype(BF)
    fr, fi = fspec[:, 0:TOKENS], fspec[:, TOKENS:] * sign
    for j in range(2):
        rows = slice(j * four, (j + 1) * four)
        xr, xi = spec[rows, 0:TOKENS], spec[rows, TOKENS:]
        prod[rows, 0:TOKENS] = (fr * xr - fi * xi).astype(BF)
        prod[rows, TOKENS:] = (fr * xi + fi * xr).astype(BF)
    cross = pltpu.make_async_remote_copy(
        src_ref=sx,
        dst_ref=rx,
        send_sem=send_sem.at[3],
        recv_sem=recv_sem.at[3],
        device_id={"dp": dp, "ctx": partner},
        device_id_type=MESH,
    )
    cross.start()
    backward(ROWS)
    y[...] = dot(wt[...], u[...]).astype(BF)

    home = pl.ds(pl.multiple_of(chip * ROWS + parity * 4, 4), 4)

    def send_out(j, carry):
        for part in range(2):
            pltpu.make_async_remote_copy(
                src_ref=y.at[pl.ds(pl.multiple_of(j * ROWS + 4 * part, 4), 4), :],
                dst_ref=out_h.at[core, home, :],
                send_sem=send_sem.at[4],
                recv_sem=recv_sem.at[4],
                device_id={"dp": far + part, "ctx": j},
                device_id_type=MESH,
            ).start()
        return carry

    lax.fori_loop(0, nb, send_out, 0)

    cross.wait()
    ours = pl.multiple_of(core * two, two)
    real, imag = None, None
    for j in range(2):
        rows = pl.ds(four * j + ours, two)
        xr, xi = spec[rows, 0:TOKENS], spec[rows, TOKENS:]
        gr = rx[j * two : (j + 1) * two, 0:TOKENS].astype(F32)
        gi = rx[j * two : (j + 1) * two, TOKENS:].astype(F32)
        re, im = xr * gr + xi * gi, xr * gi - xi * gr
        real, imag = (re, im) if j == 0 else (real + re, imag + im)
    prod[0:two, 0:TOKENS] = real.astype(BF)
    prod[0:two, TOKENS:] = (imag * sign).astype(BF)
    backward(2)
    fgs[...] = dot(wtf[...], u[0 : 2 * wide, :]).astype(BF)
    slot = pl.ds(pl.multiple_of((2 * rank + core) * piece, piece), piece)
    self_piece = pltpu.make_async_copy(
        fgs.at[pl.ds(pl.multiple_of(dp * piece, piece), piece), :], fgr_h.at[slot, :], in_sem.at[2]
    )

    @pl.when(holder)
    def _():
        self_piece.start()

    for i in range(groups):
        peer = lax.rem(dp + i, groups)

        @pl.when((peer != dp) | jnp.logical_not(holder))
        def _():
            pltpu.make_async_remote_copy(
                src_ref=fgs.at[pl.ds(pl.multiple_of(peer * piece, piece), piece), :],
                dst_ref=fgr_h.at[slot, :],
                send_sem=send_sem.at[5],
                recv_sem=recv_sem.at[5],
                device_id={"dp": peer, "ctx": 2 * chip + parity},
                device_id_type=MESH,
            ).start()

    most = fgs.at[pl.ds(0, (groups - 1) * piece), :]

    @pl.when(holder)
    def _():
        self_piece.wait()
        swap.wait_send()
        wait_bytes(fb.at[pl.ds(0, (groups // 2 - 1) * chunk), :], send_sem.at[0])
        wait_bytes(most, send_sem.at[5])
        wait_bytes(most, recv_sem.at[5])

    @pl.when(jnp.logical_not(holder))
    def _():
        wait_bytes(fb.at[pl.ds(0, (groups // 2) * chunk), :], send_sem.at[0])
        wait_bytes(fgs, send_sem.at[5])
        wait_bytes(fgs, recv_sem.at[5])

    wait_bytes(xs.at[1], send_sem.at[1])
    wait_bytes(y, send_sem.at[4])
    wait_bytes(y, recv_sem.at[4])


def last_kernel(own, groups, pre, val, post, cot, back, fgr, mixed, pre_grad, value_grad, post_grad, filter_grad):
    conv = back[0].astype(F32)
    mixed[...] = (post[...].astype(F32) * conv).astype(BF)
    post_grad[...] = (cot[...].astype(F32) * conv).astype(BF)
    grad = back[1].astype(F32)
    pre_grad[...] = (grad * val[...].astype(F32)).astype(BF)
    value_grad[...] = (grad * pre[...].astype(F32)).astype(BF)
    rows = own * 4
    total = fgr[0:rows, :].astype(F32)
    for i in range(1, groups // 2):
        total = total + fgr[i * rows : (i + 1) * rows, :].astype(F32)
    for side in range(2):
        for i in range(own):
            at = (side * own + i) * 2
            filter_grad[2 * side : 2 * side + 2, i * TOKENS : (i + 1) * TOKENS] = total[at : at + 2, :]


def body(pre_gate, values, post_gate, filters, cotangent):
    nb = lax.axis_size("ctx")
    groups = lax.axis_size("dp")
    own = nb // groups
    rows = nb * 4
    consts = tables(nb, groups)
    anywhere = pl.BlockSpec(memory_space=pl.ANY)
    vmem = pl.BlockSpec(memory_space=pltpu.VMEM)
    sig = (rows, TOKENS)
    scratch = [
        pltpu.VMEM(sig, BF), pltpu.VMEM(sig, BF), pltpu.VMEM(sig, BF), pltpu.VMEM(sig, BF),
        pltpu.VMEM(filters.shape, F32),
        *[pltpu.VMEM(c.shape, BF) for c in consts[:6]],
        pltpu.VMEM(consts[6].shape, F32),
        pltpu.VMEM((2,) + sig, BF),
        pltpu.VMEM((nb * ROWS, TOKENS), BF),
        pltpu.VMEM((own * 4, TOKENS), BF),
        pltpu.VMEM((nb * 4, TOKENS), BF),
        pltpu.VMEM((ROWS * 2 * nb, nb * ROWS), BF),
        pltpu.VMEM((nb * ROWS, ROWS * 2 * nb), BF),
        pltpu.VMEM((4 * 2 * nb, nb * 4), BF),
        pltpu.VMEM((nb * 2, 2 * 2 * nb), BF),
        pltpu.VMEM((ROWS * 2 * nb, TOKENS), F32),
        pltpu.VMEM((ROWS * nb, 2 * TOKENS), BF),
        pltpu.VMEM((ROWS * nb, 2 * TOKENS), F32),
        pltpu.VMEM((4 * nb, 2 * TOKENS), F32),
        pltpu.VMEM((ROWS * nb, 2 * TOKENS), BF),
        pltpu.VMEM((ROWS * 2 * nb, TOKENS), BF),
        pltpu.VMEM((nb * ROWS, TOKENS), BF),
        pltpu.VMEM((4 * nb, 2 * TOKENS), BF),
        pltpu.VMEM((4 * nb, 2 * TOKENS), BF),
        pltpu.VMEM((nb * 2, TOKENS), BF),
        pltpu.SemaphoreType.DMA((12,)),
        pltpu.SemaphoreType.DMA((6,)),
        pltpu.SemaphoreType.DMA((6,)),
        pltpu.SemaphoreType.DMA((nb,)),
    ]
    back, fgr = pl.pallas_call(
        functools.partial(main_kernel, nb, groups),
        out_shape=(jax.ShapeDtypeStruct((2,) + sig, BF), jax.ShapeDtypeStruct((nb * 2, TOKENS), BF)),
        in_specs=[anywhere] * 12,
        out_specs=(anywhere, anywhere),
        scratch_shapes=scratch,
        compiler_params=pltpu.CompilerParams(collective_id=0, has_side_effects=True),
        name="long_conv",
    )(pre_gate, values, post_gate, cotangent, filters, *consts)
    shape = jax.ShapeDtypeStruct(pre_gate.shape, BF)
    mixed, pre_grad, value_grad, post_grad, filter_grad = pl.pallas_call(
        functools.partial(last_kernel, own, groups),
        out_shape=(shape, shape, shape, shape, jax.ShapeDtypeStruct(filters.shape, F32)),
        in_specs=[vmem] * 6,
        out_specs=(vmem,) * 5,
        name="gates",
    )(pre_gate, values, post_gate, cotangent, back, fgr)
    return (mixed, pre_grad, value_grad, post_grad, filter_grad)


def solution(mesh):
    big = P("dp", "ctx")
    return jax.shard_map(
        body,
        mesh=mesh,
        in_specs=(big, big, big, P("ctx", "dp"), big),
        out_specs=(big, big, big, big, P("ctx", "dp")),
        check_vma=False,
    )
```

time: 61.7 us -> 57.8 us (0.937); the launches traced: 60.5 us -> 57.4 us
  Pallas kernels: 59.9 us -> 56.7 us
    pallas_call x1, Pallas kernels: 57.8 us -> 54.7 us  [body(): pl.pallas_call(functools.partial(main_kernel, nb, groups), out_shape=(jax...]
where the time goes in v3:
time: 57.8 us; the launch traced here: 57.4 us
  Pallas kernels  56.7 us (98%)
  between operations  0.64 us (1%)
    pallas_call x1, Pallas kernels, body(): pl.pallas_call(functools.partial(main_kernel, nb, groups), out_shape=(jax...  54.7 us
    pallas_call x1, Pallas kernels, body(): pl.pallas_call(functools.partial(last_kernel, own, groups), out_shape=(sh...  2.04 us

profile of v3, /device:TPU:6, one launch (start us, length us, event | category | flops | bytes accessed | tf_op | source)
XLA Modules:
  0.0 57.4 jit_solution(11817840462155575455)
XLA Ops:
  0.6 54.7 %long_conv.1 = (bf16[2,256,256]{2,1,0:T(8,128)(2,1)}, bf16[128,256]{1,0:T(8,128)(2,1)}) custom-call(bf16[256,256]{1,0:T(8,128)(2,1)} %pre.1, bf16[256,256]{1,0:T(8,128)(2,1)} %val.1, bf16[256,256]{1,0:T(8,128)(2,1)} %post.1, bf16[256,256]{1,0:T(8,128)(2,1)} %cot.1, f32[4,2048]{1,0:T(4,128)} %filt_h.1, bf16[128,512]{1,0:T(8,128)(2,1)} %constant.14.clone.e_h, ...), custom_call_target="tpu_custom_call" | custom-call | tf_op jit(solution)/shard_map/long_conv/pallas_call | solution.py:374
  55.3 2.0 %gates.1 = (bf16[256,256]{1,0:T(8,128)(2,1)}, bf16[256,256]{1,0:T(8,128)(2,1)}, bf16[256,256]{1,0:T(8,128)(2,1)}, bf16[256,256]{1,0:T(8,128)(2,1)}, f32[4,2048]{1,0:T(4,128)}) custom-call(bf16[256,256]{1,0:T(8,128)(2,1)} %pre.1, bf16[256,256]{1,0:T(8,128)(2,1)} %val.1, bf16[256,256]{1,0:T(8,128)(2,1)} %post.1, bf16[256,256]{1,0:T(8,128)(2,1)} %cot.1, ...), custom_call_target="tpu_custom_call" | custom-call | tf_op jit(solution)/shard_map/gates/pallas_call | solution.py:384
